TPU v7x, 1024 devices: a whole 4x4x32 slice. The times are simulated.
1024 devices in a mesh: seq: 64 (over z, y_hi), head: 16 (over x, y_lo, core).
Axes of the slice: x: 4, y: 4 (y_hi: 2, y_lo: 2; y = y_hi * 2 + y_lo), z: 32, core: 2. Of those that a mesh axis runs over, the one named last changes fastest.
Arguments:
- q_in: bfloat16 [8192, 2048], P(('seq', 'head')), may hold values from -52 to 52
- k_in: bfloat16 [8192, 2048], P(('seq', 'head')), may hold values from -6 to 6
- v_in: bfloat16 [8192, 2048], P(('seq', 'head')), may hold values from -6 to 6
- grad_out: bfloat16 [8192, 2048], P(('seq', 'head')), may hold values from -6 to 6
- positions: int32 [3, 8192], P(None, 'seq'), may hold values from 0 to 79, as said below
- views: int32 [8192], replicated, may hold values from 0 to 5, as said below
- adjacency: int32 [6, 2], replicated, may hold values from 0 to 5, as said below
Outputs:
- attended: bfloat16 [8192, 2048], P('seq', 'head')
- grad_q: bfloat16 [8192, 2048], P('seq', 'head')
- grad_k: bfloat16 [8192, 2048], P('seq', 'head')
- grad_v: bfloat16 [8192, 2048], P('seq', 'head')
Inputs may be any that keep to these rules, and one draw needn't show every extreme that they name: `positions`: time ids lie below 16, height ids below 44, width ids below 80. `views`: never decreasing, starting at 0; a view changes only at a multiple of 128 rows; each view holds the rows of 10 devices or of one device more, and which views hold one more is drawn. `adjacency`: the two entries of a view are distinct other views; the relation is symmetric and joins all views in one closed cycle.
All inputs are finite; a program needn't handle non-finite values.
Results may differ from a plain program's by a relative error of at most 0.025.
Values may be sent and summed in bfloat16 or wider, within the bound.
A program may use at most 32 MiB of HBM per device.

v0:
```python
import jax
import jax.numpy as jnp
from jax import lax
from jax.sharding import PartitionSpec as P

HD = 128


NEG = -1e30
THETA = 10000.0


def rope_tables(positions, width):
    side = width // 6 * 2
    first = width - 2 * side
    parts = []
    for row, group in ((0, first), (1, side), (2, side)):
        steps = jnp.arange(group // 2, dtype=jnp.float32)
        inverse = THETA ** (-2.0 * steps / group)
        parts.append(positions[row].astype(jnp.float32)[:, None] * inverse[None, :])
    angles = jnp.concatenate(parts, axis=1)
    return (jnp.cos(angles), jnp.sin(angles))


def rotate(values, cosine, sine, sign):
    half = values.shape[-1] // 2
    first = values[..., :half]
    second = values[..., half:]
    return jnp.concatenate(
        [first * cosine - sign * second * sine, sign * first * sine + second * cosine], axis=-1
    )


def neighbours(view_ids, adjacency):
    count = adjacency.shape[0]
    match = view_ids[:, None] == jnp.arange(count, dtype=jnp.int32)[None, :]
    near_one = jnp.sum(jnp.where(match, adjacency[None, :, 0], 0), axis=1)
    near_two = jnp.sum(jnp.where(match, adjacency[None, :, 1], 0), axis=1)
    return (near_one, near_two)


def in_blocks(pieces, carry, step):
    count = pieces[0].shape[0]
    size = count
    while size > 1024 and size % 2 == 0:
        size = size // 2
    number = count // size
    shaped = tuple((piece.reshape((number, size) + piece.shape[1:]) for piece in pieces))
    firsts = size * jnp.arange(number, dtype=jnp.int32)

    def advance(state, item):
        return (step(state, item[0], item[1]), None)

    final, _ = lax.scan(advance, carry, (shaped, firsts))
    return final


def on_device(q_in, k_in, v_in, grad_out, positions, views, adjacency):
    query, keys, values, grads = (
        lax.all_to_all(q_in, "head", split_axis=1, concat_axis=0, tiled=True),
        lax.all_to_all(k_in, "head", split_axis=1, concat_axis=0, tiled=True),
        lax.all_to_all(v_in, "head", split_axis=1, concat_axis=0, tiled=True),
        lax.all_to_all(grad_out, "head", split_axis=1, concat_axis=0, tiled=True),
    )
    rows, width = query.shape
    heads = width // HD
    scale = HD ** (-0.5)
    cosine, sine = rope_tables(positions, HD)
    cosine = cosine[:, None, :]
    sine = sine[:, None, :]
    query_rot = rotate(
        query.reshape(rows, heads, HD).astype(jnp.float32), cosine, sine, 1.0
    ).astype(jnp.bfloat16)
    key_rot = rotate(keys.reshape(rows, heads, HD).astype(jnp.float32), cosine, sine, 1.0).astype(
        jnp.bfloat16
    )
    value_split = values.reshape(rows, heads, HD)
    grad_split = grads.reshape(rows, heads, HD)
    first_row = lax.axis_index("seq") * rows
    own_views = lax.dynamic_slice_in_dim(views, first_row, rows)
    near_one, near_two = neighbours(own_views, adjacency)
    every_one, every_two = neighbours(views, adjacency)

    def allowed_keys(start, count):
        other = lax.dynamic_slice_in_dim(views, start, count)[None, :]
        return (
            (other == own_views[:, None])
            | (other == near_one[:, None])
            | (other == near_two[:, None])
        )

    def scores_for(key_block, allow):
        scores = (
            jnp.einsum("qhd,khd->hqk", query_rot, key_block, preferred_element_type=jnp.float32)
            * scale
        )
        return jnp.where(allow[None], scores, NEG)

    def soft_update(top, total, accum, block, start):
        key_block, value_block = block
        allow = allowed_keys(start, key_block.shape[0])
        scores = scores_for(key_block, allow)
        new_top = jnp.maximum(top, jnp.max(scores, axis=2))
        shrink = jnp.exp(top - new_top)
        weights = jnp.where(allow[None], jnp.exp(scores - new_top[..., None]), 0.0)
        total = total * shrink + jnp.sum(weights, axis=2)
        accum = accum * shrink[..., None] + jnp.einsum(
            "hqk,khd->hqd",
            weights.astype(jnp.bfloat16),
            value_block,
            preferred_element_type=jnp.float32,
        )
        return (new_top, total, accum, weights, shrink)

    top_init = jnp.full((heads, rows), NEG, jnp.float32)
    total_init = jnp.zeros((heads, rows), jnp.float32)
    accum_init = jnp.zeros((heads, rows, HD), jnp.float32)

    def step(inner, block, bstart):
        top, total, accum, weights, shrink = soft_update(
            inner[0], inner[1], inner[2], block, bstart
        )
        return (top, total, accum)

    top, total, accum = in_blocks(
        (
            lax.all_gather(key_rot, "seq", axis=0, tiled=True),
            lax.all_gather(value_split, "seq", axis=0, tiled=True),
        ),
        (top_init, total_init, accum_init),
        step,
    )
    output = accum / total[..., None]
    finish_level = top + jnp.log(total)
    finish_delta = jnp.sum(
        grad_split.astype(jnp.float32) * jnp.transpose(output, (1, 0, 2)), axis=2
    ).T
    output, level, delta = (output, finish_level, finish_delta)

    def step(inner, block, bstart):
        key_block, value_block = block
        allow = allowed_keys(bstart, key_block.shape[0])
        scores = scores_for(key_block, allow)
        probs = jnp.where(allow[None], jnp.exp(scores - level[..., None]), 0.0)
        dprobs = jnp.einsum(
            "qhd,khd->hqk", grad_split, value_block, preferred_element_type=jnp.float32
        )
        dscores = (probs * (dprobs - delta[..., None])).astype(jnp.bfloat16)
        return inner + jnp.einsum(
            "hqk,khd->hqd", dscores, key_block, preferred_element_type=jnp.float32
        )

    grad_query = (
        in_blocks(
            (
                lax.all_gather(key_rot, "seq", axis=0, tiled=True),
                lax.all_gather(value_split, "seq", axis=0, tiled=True),
            ),
            accum_init,
            step,
        )
        * scale
    )
    level_all, delta_all = (
        lax.all_gather(level.T, "seq", axis=0, tiled=True),
        lax.all_gather(delta.T, "seq", axis=0, tiled=True),
    )

    def step(inner, block, bstart):
        grad_key, grad_value = inner
        query_block, grad_block = block
        count = query_block.shape[0]
        query_views = lax.dynamic_slice_in_dim(views, bstart, count)[None, :]
        query_one = lax.dynamic_slice_in_dim(every_one, bstart, count)[None, :]
        query_two = lax.dynamic_slice_in_dim(every_two, bstart, count)[None, :]
        mine = own_views[:, None]
        allow = (mine == query_views) | (mine == query_one) | (mine == query_two)
        level_block = lax.dynamic_slice_in_dim(level_all, bstart, count).T
        delta_block = lax.dynamic_slice_in_dim(delta_all, bstart, count).T
        scores = (
            jnp.einsum("khd,qhd->hkq", key_rot, query_block, preferred_element_type=jnp.float32)
            * scale
        )
        probs = jnp.where(allow[None], jnp.exp(scores - level_block[:, None, :]), 0.0)
        grad_value = grad_value + jnp.einsum(
            "hkq,qhd->hkd",
            probs.astype(jnp.bfloat16),
            grad_block,
            preferred_element_type=jnp.float32,
        )
        dprobs = jnp.einsum(
            "khd,qhd->hkq", value_split, grad_block, preferred_element_type=jnp.float32
        )
        dscores = (probs * (dprobs - delta_block[:, None, :])).astype(jnp.bfloat16)
        grad_key = grad_key + jnp.einsum(
            "hkq,qhd->hkd", dscores, query_block, preferred_element_type=jnp.float32
        )
        return (grad_key, grad_value)

    grad_key, grad_value = in_blocks(
        (
            lax.all_gather(query_rot, "seq", axis=0, tiled=True),
            lax.all_gather(grad_split, "seq", axis=0, tiled=True),
        ),
        (accum_init, accum_init),
        step,
    )

    def token_major(stack):
        return jnp.transpose(stack, (1, 0, 2))

    attended = token_major(output).reshape(rows, width).astype(jnp.bfloat16)
    grad_q = (
        rotate(token_major(grad_query), cosine, sine, -1.0)
        .reshape(rows, width)
        .astype(jnp.bfloat16)
    )
    grad_k = (
        rotate(token_major(grad_key) * scale, cosine, sine, -1.0)
        .reshape(rows, width)
        .astype(jnp.bfloat16)
    )
    grad_v = token_major(grad_value).reshape(rows, width).astype(jnp.bfloat16)
    return (attended, grad_q, grad_k, grad_v)


def solution(mesh):
    in_specs = (
        P(("seq", "head"), None),
        P(("seq", "head"), None),
        P(("seq", "head"), None),
        P(("seq", "head"), None),
        P(None, "seq"),
        P(),
        P(),
    )
    out_specs = (P("seq", "head"), P("seq", "head"), P("seq", "head"), P("seq", "head"))
    return jax.shard_map(
        on_device, mesh=mesh, in_specs=in_specs, out_specs=out_specs, check_vma=False
    )
```

profile of v0, /device:TPU:6, one launch (start us, length us, event | category | flops | bytes accessed | tf_op | source)
XLA Modules:
  0.0 1200.1 jit_solution(7928688031974726790)
XLA Ops:
  7.2 16.5 %all-to-all-start.1 = ((bf16[8,16,128]{2,0,1:T(8,128)(2,1)}), bf16[8,16,128]{2,0,1:T(8,128)(2,1)S(1)}, u32[]{:S(2)}, u32[]{:S(2)}) async-start(bf16[8,16,128]{2,0,1:T(8,128)(2,1)} %bitcast.265), calls=%async_computation.1 | async-start | bytes 65536 | tf_op jit(solution)/shard_map/all_to_all | solution.py:60
  24.7 3.1 all-to-all-done.1
  27.7 5.5 all-to-all-start
  33.6 3.7 all-to-all-done
  38.2 10.2 all_to_all.58
  49.2 5.5 all-to-all-start.3
  59.4 253.5 %all-gather.8.cloned.1.call-done = bf16[8192,1,128]{2,0,1:T(8,128)(2,1)} async-done(((bf16[128,1,128]{2,0,1:T(8,128)(2,1)}), bf16[8192,1,128]{2,0,1:T(8,128)(2,1)}) %all-gather.8.cloned.1.call-update) | async-done | bytes 2097168 | tf_op jit(solution)/shard_map/all_gather | solution.py:127
  312.9 271.0 %all-gather.10.cloned.1.call-done = bf16[8192,1,128]{2,0,1:T(8,128)(2,1)} async-done(((bf16[128,1,128]{2,0,1:T(8,128)(2,1)}), bf16[8192,1,128]{2,0,1:T(8,128)(2,1)}) %all-gather.10.cloned.1.call-update) | async-done | bytes 2097168 | tf_op jit(solution)/shard_map/all_gather | solution.py:128
  583.9 50.4 %while.39 = (s32[]{:T(128)}, f32[1,128]{1,0:T(1,128)S(1)}, f32[1,128]{1,0:T(1,128)S(1)}, f32[1,128,128]{2,1,0:T(8,128)S(1)}, s32[8]{0:T(128)S(1)}, /*index=5*/s3...) while((s32[]{:T(128)}, f32[1,128]{1,0:T(1,128)S(1)}, ...), condition=%wide.region_5.6_spmd.clone, body=%wide.region_2.0_spmd.clone.sunk | while | flops 70304512 | bytes 2295499 | solution.py:54
  635.2 142.0 %all-gather.2 = f32[64,1,128]{2,1,0:T(1,128)S(1)} all-gather(f32[1,1,128]{2,1,0:T(1,128)S(1)} %bitcast.269), channel_id=3, replica_groups=mesh['seq'=64,'head'=16] {'seq'}, dimensions={0}, use_global_device_ids=true | all-gather | bytes 33280 | tf_op jit(solution)/shard_map/all_gather | solution.py:166
  777.2 142.1 %all-gather = f32[1,8192]{1,0:T(1,128)S(1)} all-gather(f32[1,128]{1,0:T(1,128)S(1)} %log_add_fusion), channel_id=2, replica_groups=mesh['seq'=64,'head'=16] {'seq'}, dimensions={1}, use_global_device_ids=true | all-gather | bytes 33280 | tf_op jit(solution)/shard_map/all_gather | solution.py:165
  919.3 49.0 %while.40 = (s32[]{:T(128)}, f32[1,128,128]{2,1,0:T(8,128)S(1)}, s32[8]{0:T(128)S(1)}, s32[8192]{0:T(1024)}, s32[128]{0:T(128)S(1)}, /*index=5*/s32[128]{0:T(128...) while((s32[]{:T(128)}, f32[1,128,128]{2,1,0:T(8,128)S(1)}, ...), condition=%wide.region_8.9_spmd.clone, body=%wide.region_7.8_spmd.clone.sunk | while | flops 102268928 | bytes 2048209 | solution.py:54
  923.8 1.6 fusion.131
  929.9 1.6 fusion.131
  936.0 1.6 fusion.131
  942.1 1.7 fusion.131
  948.3 1.6 fusion.131
  954.4 1.6 fusion.131
  960.5 1.6 fusion.131
  966.6 1.6 fusion.131
  968.3 158.7 %all-gather.14.cloned.1.call-done = bf16[8192,1,128]{2,0,1:T(8,128)(2,1)} async-done(((bf16[128,1,128]{2,0,1:T(8,128)(2,1)}), bf16[8192,1,128]{2,0,1:T(8,128)(2,1)}) %all-gather.14.cloned.1.call-update) | async-done | bytes 2097168 | tf_op jit(solution)/shard_map/all_gather | solution.py:203
  1127.1 65.0 %while.41 = (s32[]{:T(128)}, f32[1,128,128]{2,1,0:T(8,128)S(1)}, f32[1,128,128]{2,1,0:T(8,128)S(1)}, s32[128]{0:T(128)S(1)}, s32[8]{0:T(128)S(1)}, /*index=5*/s3...) while((s32[]{:T(128)}, f32[1,128,128]{2,1,0:T(8,128)S(1)}, ...), condition=%wide.region_12.13_spmd.clone, body=%wide.region_11.12_spmd.clone.sunk | while | flops 135856128 | bytes 3013350 | solution.py:54
  1130.6 1.8 fusion.139
  1138.7 1.8 fusion.139
  1146.9 1.8 fusion.139
  1155.0 1.8 fusion.139
  1158.0 1.5 fusion.140
  1163.1 1.8 fusion.139
  1171.3 1.8 fusion.139
  1174.3 1.5 fusion.140
  1179.4 1.8 fusion.139
  1187.5 1.8 fusion.139
  (190 shorter events, 97.8 us)
Async XLA Ops:
  7.2 20.6 %all-to-all-start.1 = ((bf16[8,16,128]{2,0,1:T(8,128)(2,1)}), bf16[8,16,128]{2,0,1:T(8,128)(2,1)S(1)}, u32[]{:S(2)}, u32[]{:S(2)}) async-start(bf16[8,16,128]{2,0,1:T(8,128)(2,1)} %bitcast.265), calls=%async_computation.1 | async-start | bytes 65536 | tf_op jit(solution)/shard_map/all_to_all | solution.py:60
  27.7 9.6 all-to-all-start
  33.2 279.7 %all-gather.8.cloned.1.call-start = ((), (), s32[]{:S(2)}) async-start(), calls=%async_computation.4 | async-start | bytes 2129920 | tf_op jit(solution)/shard_map/all_gather | solution.py:127
  38.1 545.8 %all-gather.10.cloned.1.call-start = ((), (), s32[]{:S(2)}) async-start(), calls=%async_computation.5 | async-start | bytes 2129920 | tf_op jit(solution)/shard_map/all_gather | solution.py:128
  48.4 919.9 %all-gather.12.cloned.1.call-start = ((), (), s32[]{:S(2)}) async-start(), calls=%async_computation.6 | async-start | bytes 2129920 | tf_op jit(solution)/shard_map/all_gather | solution.py:202
  49.2 9.6 all-to-all-start.3
  54.7 1072.4 %all-gather.14.cloned.1.call-start = ((), (), s32[]{:S(2)}) async-start(), calls=%async_computation.7 | async-start | bytes 2129920 | tf_op jit(solution)/shard_map/all_gather | solution.py:203
  58.8 0.6 copy-start
  583.9 51.1 %copy-start.1 = (bf16[8,16,128]{2,0,1:T(8,128)(2,1)S(1)}, bf16[8,16,128]{2,0,1:T(8,128)(2,1)}, u32[]{:S(2)}) copy-start(bf16[8,16,128]{2,0,1:T(8,128)(2,1)} %copy-done) | copy-start | bytes 98308
  919.3 207.8 %copy-start.2 = (bf16[8,16,128]{2,0,1:T(8,128)(2,1)S(1)}, bf16[8,16,128]{2,0,1:T(8,128)(2,1)}, u32[]{:S(2)}) copy-start(bf16[8,16,128]{2,0,1:T(8,128)(2,1)} %all_to_all.58) | copy-start | bytes 98308
  919.3 207.8 %copy-start.3 = (bf16[128,1,128]{2,0,1:T(8,128)(2,1)S(1)}, bf16[128,1,128]{2,0,1:T(8,128)(2,1)}, u32[]{:S(2)}) copy-start(bf16[128,1,128]{2,0,1:T(8,128)(2,1)} %pad_maximum_fusion.1) | copy-start | bytes 98308
Sparse Core Ops, SparseCore 0:
  38.8 274.0 all-gather.7
  317.2 266.6 all-gather.9
  588.8 266.7 all-gather.11
  860.2 266.8 all-gather.13
where the time goes:
time: 1200 us
  waiting for transfers between devices  691 us (58%)
  blocking collectives  294 us (24%)
  matrix products  80.4 us (7%)
  loops' own time  46.4 us (4%)
  local copies, waits for them, and re-layouts  37.8 us (3%)
  starting transfers between devices  27.6 us (2%)
  between operations  13.9 us (1%)
    all_gather x1, waiting for transfers between devices, on_device(): lax.all_gather(value_split, 'seq', axis=0, tiled=True)  271 us
    all_gather x1, waiting for transfers between devices, on_device(): lax.all_gather(key_rot, 'seq', axis=0, tiled=True)  254 us
    all_gather x1, waiting for transfers between devices, on_device(): lax.all_gather(grad_split, 'seq', axis=0, tiled=True)  159 us
    all_gather x1, blocking collectives, on_device(): lax.all_gather(level.T, 'seq', axis=0, tiled=True)  142 us
    all_gather x1, blocking collectives, on_device(): lax.all_gather(delta.T, 'seq', axis=0, tiled=True)  142 us
    another operation x3, loops' own time, in_blocks(): final, _ = lax.scan(advance, carry, (shaped, firsts))  46.4 us
  transfers between devices with their start and end apart: 7, of which 6 were waited for; matrix products, arithmetic and copies ran while one was open for 6% of the time, Pallas kernels for 0%

commit v1 on v0

v1 whole, which is shorter than its diff:
```python
import functools

import jax
import jax.numpy as jnp
from jax import lax
from jax.experimental import pallas as pl
from jax.experimental.pallas import tpu as pltpu
from jax.sharding import PartitionSpec as P

HD = 128
NEG = -1e30
THETA = 10000.0
MESH = pl.DeviceIdType.MESH
SKEW = 1


def rope_tables(positions, width):
    side = width // 6 * 2
    first = width - 2 * side
    parts = []
    for row, group in ((0, first), (1, side), (2, side)):
        steps = jnp.arange(group // 2, dtype=jnp.float32)
        inverse = THETA ** (-2.0 * steps / group)
        parts.append(positions[row].astype(jnp.float32)[:, None] * inverse[None, :])
    angles = jnp.concatenate(parts, axis=1)
    return (jnp.cos(angles), jnp.sin(angles))


def rotate(values, cosine, sine, sign):
    half = values.shape[-1] // 2
    first = values[..., :half]
    second = values[..., half:]
    return jnp.concatenate(
        [first * cosine - sign * second * sine, sign * first * sine + second * cosine], axis=-1
    )


def dot_nt(a, b):
    return lax.dot_general(a, b, (((1,), (1,)), ((), ())), preferred_element_type=jnp.float32)


def dot_nn(a, b):
    return lax.dot_general(a, b, (((1,), (0,)), ((), ())), preferred_element_type=jnp.float32)


def dot_tn(a, b):
    return lax.dot_general(a, b, (((0,), (0,)), ((), ())), preferred_element_type=jnp.float32)


def kernel(
    seq_count, toks,
    k_ref, v_ref, q_ref, d_ref, bias_ref,
    att_ref, grad_ref,
    ring, gbuf, acc, stat, racc, rstat, lring, glse, dqt, dkv, attbuf, hsend, hrecv,
    a2a_send, a2a_recv, g_send, g_recv, g_own, r_send, r_recv, l_send, l_recv,
    p_send, p_recv, gl_send, gl_recv, gl_own, at_send, at_recv, h_send, h_recv,
):
    T = toks
    SUB = T // 16
    NP = seq_count // 4
    HALF = NP // 2
    scale = HD ** (-0.5)
    s = lax.axis_index("seq")
    hd = lax.axis_index("head")
    pair = s // 4
    r = (s // 2) % 2
    yh = s % 2
    xh = hd // 8
    xl = (hd // 4) % 2
    low = hd % 4
    j = 2 * xh + yh
    head = (2 * r + xl) * 4 + low
    base = 4 * pair
    diag = xh == r

    right = ((s + 4) % seq_count, hd)
    left = ((s + seq_count - 4) % seq_count, hd)

    def member(i):
        return (base + 2 * r + i % 2, (2 * (i // 2) + xl) * 4 + low)

    def home(i):
        return (base + i, head)

    def home_sender(i):
        return (base + 2 * xh + i % 2, (2 * (i // 2) + xl) * 4 + low)

    def a2a_dest(h):
        xo = h // 4
        return (base + 2 * (xo // 2) + yh, (2 * r + xo % 2) * 4 + h % 4)

    def is_me(dev):
        return jnp.logical_and(dev[0] == s, dev[1] == hd)

    barrier = pltpu.get_barrier_semaphore()

    @pl.loop(0, 16)
    def _(i):
        src = (base + j, i)

        @pl.when(jnp.logical_not(is_me(src)))
        def _():
            pl.semaphore_signal(barrier, inc=1, device_id=src, device_id_type=MESH)

    for i in range(4):
        src = home_sender(i)

        @pl.when(jnp.logical_not(is_me(src)))
        def _():
            pl.semaphore_signal(barrier, inc=1, device_id=src, device_id_type=MESH)

    for dev in (right, left):
        pl.semaphore_signal(barrier, inc=1, device_id=dev, device_id_type=MESH)
    peers = []
    for delta in (1, 2, 3):
        i = (j + delta) % 4
        peers.append(i)
        pl.semaphore_signal(barrier, inc=1, device_id=member((j - delta + 4) % 4), device_id_type=MESH)
    pl.semaphore_wait(barrier, 25 - 2 * diag.astype(jnp.int32))

    inputs = (k_ref, v_ref, q_ref, d_ref)

    def a2a_remote(t, h):
        return pltpu.make_async_remote_copy(
            src_ref=inputs[t].at[:, pl.ds(pl.multiple_of(h * HD, HD), HD)],
            dst_ref=ring.at[t, pl.ds(pl.multiple_of(hd * SUB, SUB), SUB), :],
            send_sem=a2a_send.at[t], recv_sem=a2a_recv.at[t],
            device_id=a2a_dest(h), device_id_type=MESH,
        )

    def a2a_local(t, h):
        return pltpu.make_async_copy(
            inputs[t].at[:, pl.ds(pl.multiple_of(h * HD, HD), HD)],
            ring.at[t, pl.ds(pl.multiple_of(hd * SUB, SUB), SUB), :],
            a2a_recv.at[t],
        )

    for t in range(4):
        @pl.loop(0, 16)
        def _(h):
            mine = is_me(a2a_dest(h))

            @pl.when(mine)
            def _():
                a2a_local(t, h).start()

            @pl.when(jnp.logical_not(mine))
            def _():
                a2a_remote(t, h).start()

    def rows(i):
        return pl.ds(i * T, T)

    def own(t):
        return ring.at[t, rows(0), :]

    def wait_bytes(ref, sem):
        pltpu.make_async_copy(ref, ref, sem).wait()

    def ring_copy(t, way, step):
        if way == 0:
            src = jnp.maximum(2 * step - 3, 0)
            dst = 2 * step - 1
        else:
            src = 2 * step - 2
            dst = jnp.minimum(2 * step, 2 * HALF - 1)
        return pltpu.make_async_remote_copy(
            src_ref=ring.at[t, pl.ds(pl.multiple_of(src * T, T), T), :],
            dst_ref=ring.at[t, pl.ds(pl.multiple_of(dst * T, T), T), :],
            send_sem=r_send.at[t, way, step - 1], recv_sem=r_recv.at[t, way, step - 1],
            device_id=right if way == 0 else left, device_id_type=MESH,
        )

    def lse_copy(way, step):
        if way == 0:
            src = jnp.maximum(2 * step - 3, 0)
            dst = 2 * step - 1
        else:
            src = 2 * step - 2
            dst = jnp.minimum(2 * step, 2 * HALF - 1)
        return pltpu.make_async_remote_copy(
            src_ref=lring.at[src], dst_ref=lring.at[dst],
            send_sem=l_send.at[way, step - 1], recv_sem=l_recv.at[way, step - 1],
            device_id=right if way == 0 else left, device_id_type=MESH,
        )

    def group_copy(t, n):
        return pltpu.make_async_remote_copy(
            src_ref=own(t), dst_ref=gbuf.at[t, pl.ds(pl.multiple_of(j * T, T), T), :],
            send_sem=g_send.at[t, n], recv_sem=g_recv.at[t, n],
            device_id=member(peers[n]), device_id_type=MESH,
        )

    def group_own(t):
        return pltpu.make_async_copy(
            own(t), gbuf.at[t, pl.ds(pl.multiple_of(j * T, T), T), :], g_own.at[t]
        )

    for t in (0, 1):
        wait_bytes(own(t), a2a_recv.at[t])
        for way in (0, 1):
            ring_copy(t, way, jnp.int32(1)).start()
    for t in (2, 3):
        wait_bytes(own(t), a2a_recv.at[t])
    for t in (2, 3, 0, 1):
        for n in range(3):
            group_copy(t, n).start()
        group_own(t).start()

    def group_wait(t):
        for n in range(3):
            group_copy(t, n).wait_recv()
        group_own(t).wait()

    group_wait(2)

    def fwd(start, size, bias, first):
        keys = ring[0, pl.ds(start, size), :]
        vals = ring[1, pl.ds(start, size), :]
        st = dot_nt(keys, gbuf[2]) * scale
        st = st + bias
        peak = jnp.max(st, axis=0, keepdims=True)
        if first:
            top = peak
        else:
            top = jnp.maximum(stat[0:1, :], peak)
        e = jnp.exp(st - top)
        total = jnp.sum(e, axis=0, keepdims=True)
        out = dot_tn(vals, e.astype(jnp.bfloat16))
        if first:
            stat[1:2, :] = total
            acc[...] = out
        else:
            shrink = jnp.exp(stat[0:1, :] - top)
            stat[1:2, :] = stat[1:2, :] * shrink + total
            acc[...] = acc[...] * shrink + out
        stat[0:1, :] = top

    def bias_of(step):
        one = jnp.broadcast_to(bias_ref[2 * step - 1], (T, 4 * T))
        two = jnp.broadcast_to(bias_ref[2 * step], (T, 4 * T))
        return jnp.concatenate([one, two], axis=0)

    LAST = 2 * HALF - 1
    stat[...] = jnp.zeros_like(stat)
    fwd(0, T, bias_ref[0], True)

    def forward_ring(pairs, step):
        for t, way in pairs:
            ring_copy(t, way, step).wait_recv()

            @pl.when(step + 1 < HALF)
            def _():
                ring_copy(t, way, step + 1).start()

            if (t % 2) == way:
                @pl.when(step + 1 == HALF)
                def _():
                    ring_copy(t, way, step + 1).start()

    @pl.loop(1, HALF)
    def _(step):
        forward_ring(((0, 0), (0, 1), (1, 0), (1, 1)), step)
        fwd(pl.multiple_of((2 * step - 1) * T, T), 2 * T, bias_of(step), False)

    for t in (2, 3):
        for way in (0, 1):
            ring_copy(t, way, jnp.int32(1)).start()
    ring_copy(0, 0, jnp.int32(HALF)).wait_recv()
    ring_copy(1, 1, jnp.int32(HALF)).wait_recv()
    fwd(LAST * T, T, bias_ref[LAST], False)

    def part_copy(which, n):
        lanes = pl.ds(pl.multiple_of(peers[n] * T, T), T)
        src, dst = ((acc, racc), (stat, rstat))[which]
        return pltpu.make_async_remote_copy(
            src_ref=src.at[:, lanes], dst_ref=dst.at[n],
            send_sem=p_send.at[which, n], recv_sem=p_recv.at[which, n],
            device_id=member(peers[n]), device_id_type=MESH,
        )

    for n in range(3):
        part_copy(1, n).start()
        part_copy(0, n).start()
    for t in (3, 0, 1):
        group_wait(t)
    mine = pl.ds(pl.multiple_of(j * T, T), T)
    own_stat = stat[:, mine]
    own_acc = acc[:, mine]
    for n in range(3):
        part_copy(1, n).wait_recv()
        part_copy(0, n).wait_recv()
    stats = [own_stat] + [rstat[n] for n in range(3)]
    top = stats[0][0:1]
    for item in stats[1:]:
        top = jnp.maximum(top, item[0:1])
    total = jnp.zeros_like(top)
    out = jnp.zeros_like(own_acc)
    for n, item in enumerate(stats):
        weight = jnp.exp(item[0:1] - top)
        total = total + item[1:2] * weight
        out = out + (own_acc if n == 0 else racc[n - 1]) * weight
    out = out / total
    lse = top + jnp.log(total)
    dt = jnp.transpose(ring[3, 0:T, :].astype(jnp.float32))
    delta = jnp.sum(dt * out, axis=0, keepdims=True)
    lring[0, 0:1, :] = lse
    lring[0, 1:2, :] = delta
    lring[0, 2:8, :] = jnp.zeros((6, T), jnp.float32)
    attbuf[...] = jnp.transpose(out).astype(jnp.bfloat16)
    for way in (0, 1):
        lse_copy(way, jnp.int32(1)).start()

    def glse_copy(n):
        return pltpu.make_async_remote_copy(
            src_ref=lring.at[0], dst_ref=glse.at[:, mine],
            send_sem=gl_send.at[n], recv_sem=gl_recv.at[n],
            device_id=member(peers[n]), device_id_type=MESH,
        )

    glse_own = pltpu.make_async_copy(lring.at[0], glse.at[:, mine], gl_own)
    for n in range(3):
        glse_copy(n).start()
    glse_own.start()

    def att_remote():
        return pltpu.make_async_remote_copy(
            src_ref=attbuf, dst_ref=att_ref, send_sem=at_send, recv_sem=at_recv,
            device_id=home(j), device_id_type=MESH,
        )

    att_local = pltpu.make_async_copy(attbuf, att_ref, at_recv)
    att_mine = is_me(home(j))

    @pl.when(att_mine)
    def _():
        att_local.start()

    @pl.when(jnp.logical_not(att_mine))
    def _():
        att_remote().start()

    def grad_q(start, size, bias, first):
        keys = ring[0, pl.ds(start, size), :]
        vals = ring[1, pl.ds(start, size), :]
        st = dot_nt(keys, gbuf[2]) * scale
        p = jnp.exp(st + (bias - glse[0:1, :]))
        dp = dot_nt(vals, gbuf[3])
        ds = (p * (dp - glse[1:2, :])).astype(jnp.bfloat16)
        part = dot_tn(keys, ds)
        if first:
            dqt[...] = part
        else:
            dqt[...] += part

    def grad_kv(slot, first):
        start = slot * T if isinstance(slot, int) else pl.multiple_of(slot * T, T)
        queries = ring[2, pl.ds(start, T), :]
        grads = ring[3, pl.ds(start, T), :]
        level = lring[slot, 0:1, :]
        delta = lring[slot, 1:2, :]
        st = dot_nt(gbuf[0], queries) * scale
        dp = dot_nt(gbuf[1], grads)
        bias = bias_ref[slot]
        shift = [
            jnp.broadcast_to(bias[:, i * T:(i + 1) * T] - level, (T, T)) for i in range(4)
        ]
        p = jnp.exp(st + jnp.concatenate(shift, axis=0))
        ds = (p * (dp - delta)).astype(jnp.bfloat16)
        dv = dot_nn(p.astype(jnp.bfloat16), grads)
        dk = dot_nn(ds, queries)
        if first:
            dkv[0] = dk
            dkv[1] = dv
        else:
            dkv[0] += dk
            dkv[1] += dv

    @pl.loop(1, HALF + SKEW)
    def _(step):
        @pl.when(step < HALF)
        def _():
            forward_ring(((2, 0), (2, 1), (3, 0), (3, 1)), step)

        @pl.when(step == SKEW + 1)
        def _():
            for n in range(3):
                glse_copy(n).wait_recv()
            glse_own.wait()
            grad_q(0, T, bias_ref[0], True)
            grad_q(LAST * T, T, bias_ref[LAST], False)
            grad_kv(0, True)

        @pl.when(step > SKEW)
        def _():
            at = step - SKEW
            for way in (0, 1):
                lse_copy(way, at).wait_recv()

                @pl.when(at + 1 < HALF)
                def _():
                    lse_copy(way, at + 1).start()

            @pl.when(at + 1 == HALF)
            def _():
                lse_copy(0, at + 1).start()

            grad_q(pl.multiple_of((2 * at - 1) * T, T), 2 * T, bias_of(at), False)
            grad_kv(2 * at - 1, False)
            grad_kv(2 * at, False)

    for i in range(4):
        hsend[0, i * T:(i + 1) * T, :] = (
            jnp.transpose(dqt[:, i * T:(i + 1) * T]) * scale
        ).astype(jnp.bfloat16)

    def home_remote(t, i):
        return pltpu.make_async_remote_copy(
            src_ref=hsend.at[t, rows(i), :], dst_ref=hrecv.at[t, j],
            send_sem=h_send.at[t, i], recv_sem=h_recv.at[t, j],
            device_id=home(i), device_id_type=MESH,
        )

    def home_local(t, i):
        return pltpu.make_async_copy(hsend.at[t, rows(i), :], hrecv.at[t, j], h_recv.at[t, j])

    def send_home(t):
        for i in range(4):
            here = is_me(home(i))

            @pl.when(here)
            def _():
                home_local(t, i).start()

            @pl.when(jnp.logical_not(here))
            def _():
                home_remote(t, i).start()

    send_home(0)
    ring_copy(2, 0, jnp.int32(HALF)).wait_recv()
    ring_copy(3, 1, jnp.int32(HALF)).wait_recv()
    lse_copy(0, jnp.int32(HALF)).wait_recv()
    grad_kv(LAST, False)
    hsend[1] = (dkv[0] * scale).astype(jnp.bfloat16)
    hsend[2] = dkv[1].astype(jnp.bfloat16)
    send_home(1)
    send_home(2)

    for t in range(4):
        @pl.loop(0, 16)
        def _(h):
            @pl.when(jnp.logical_not(is_me(a2a_dest(h))))
            def _():
                a2a_remote(t, h).wait_send()

        for n in range(3):
            group_copy(t, n).wait_send()

        @pl.loop(1, HALF)
        def _(step):
            for way in (0, 1):
                ring_copy(t, way, step).wait_send()

        ring_copy(t, t % 2, jnp.int32(HALF)).wait_send()

    @pl.loop(1, HALF)
    def _(step):
        for way in (0, 1):
            lse_copy(way, step).wait_send()

    lse_copy(0, jnp.int32(HALF)).wait_send()
    for n in range(3):
        part_copy(0, n).wait_send()
        part_copy(1, n).wait_send()
        glse_copy(n).wait_send()

    @pl.when(jnp.logical_not(att_mine))
    def _():
        att_remote().wait_send()

    wait_bytes(att_ref, at_recv)
    for t in range(3):
        for i in range(4):
            wait_bytes(hrecv.at[t, i], h_recv.at[t, i])
        whole = hrecv[t, 0].astype(jnp.float32)
        for i in range(1, 4):
            whole = whole + hrecv[t, i].astype(jnp.float32)
        grad_ref[t] = whole
    for t in range(3):
        for i in range(4):
            @pl.when(jnp.logical_not(is_me(home(i))))
            def _():
                home_remote(t, i).wait_send()


def exchange_and_attend(seq_count, toks, keys, values, query, grads, bias):
    NP = seq_count // 4
    HALF = NP // 2
    T = toks
    bf, f32 = jnp.bfloat16, jnp.float32
    dma = pltpu.SemaphoreType.DMA
    vmem = pl.BlockSpec(memory_space=pltpu.VMEM)
    return pl.pallas_call(
        functools.partial(kernel, seq_count, toks),
        out_shape=(
            jax.ShapeDtypeStruct((T, HD), bf),
            jax.ShapeDtypeStruct((3, T, HD), f32),
        ),
        in_specs=[vmem] * 5,
        out_specs=(vmem, vmem),
        scratch_shapes=[
            pltpu.VMEM((4, NP * T, HD), bf),
            pltpu.VMEM((4, 4 * T, HD), bf),
            pltpu.VMEM((HD, 4 * T), f32),
            pltpu.VMEM((8, 4 * T), f32),
            pltpu.VMEM((3, HD, T), f32),
            pltpu.VMEM((3, 8, T), f32),
            pltpu.VMEM((NP, 8, T), f32),
            pltpu.VMEM((8, 4 * T), f32),
            pltpu.VMEM((HD, 4 * T), f32),
            pltpu.VMEM((2, 4 * T, HD), f32),
            pltpu.VMEM((T, HD), bf),
            pltpu.VMEM((3, 4 * T, HD), bf),
            pltpu.VMEM((3, 4, T, HD), bf),
            dma((4,)), dma((4,)),
            dma((4, 3)), dma((4, 3)), dma((4,)),
            dma((4, 2, HALF)), dma((4, 2, HALF)),
            dma((2, HALF)), dma((2, HALF)),
            dma((2, 3)), dma((2, 3)),
            dma((3,)), dma((3,)), dma,
            dma, dma,
            dma((3, 4)), dma((3, 4)),
        ],
        compiler_params=pltpu.CompilerParams(collective_id=0, has_side_effects=True),
    )(keys, values, query, grads, bias)


def on_device(seq_count, q_in, k_in, v_in, grad_out, positions, views, adjacency):
    NP = seq_count // 4
    HALF = NP // 2
    T = positions.shape[1]
    sub = q_in.shape[0]
    s = lax.axis_index("seq")
    hd = lax.axis_index("head")
    cosine, sine = rope_tables(positions, HD)
    own_pos = lax.dynamic_slice_in_dim(positions, hd * sub, sub, axis=1)
    c8, s8 = rope_tables(own_pos, HD)

    def turn(x):
        y = rotate(x.reshape(sub, -1, HD).astype(jnp.float32), c8[:, None], s8[:, None], 1.0)
        return y.astype(jnp.bfloat16).reshape(x.shape)

    pair = s // 4
    j = 2 * (hd // 8) + s % 2
    step = jnp.arange(NP, dtype=jnp.int32)
    offset = jnp.where(step % 2 == 1, -(step + 1) // 2, step // 2)
    other = (pair + offset + NP) % NP * 4 + j
    mine = 4 * pair + jnp.arange(4, dtype=jnp.int32)
    block_views = views.reshape(seq_count, T)[:, 0]
    every = jnp.arange(seq_count, dtype=jnp.int32)

    def view_of(index):
        return jnp.sum(jnp.where(index[:, None] == every[None, :], block_views[None, :], 0), axis=1)

    key_view = view_of(other)
    own_view = view_of(mine)
    match = own_view[:, None] == jnp.arange(adjacency.shape[0], dtype=jnp.int32)[None, :]
    near_one = jnp.sum(jnp.where(match, adjacency[None, :, 0], 0), axis=1)
    near_two = jnp.sum(jnp.where(match, adjacency[None, :, 1], 0), axis=1)
    allow = (
        (key_view[:, None] == own_view[None, :])
        | (key_view[:, None] == near_one[None, :])
        | (key_view[:, None] == near_two[None, :])
    )
    bias = jnp.broadcast_to(jnp.where(allow, 0.0, NEG)[:, :, None], (NP, 4, T)).reshape(NP, 1, 4 * T)

    attended, grads = exchange_and_attend(
        seq_count, T, turn(k_in), v_in, turn(q_in), grad_out, bias
    )
    grad_q = rotate(grads[0], cosine, sine, -1.0).astype(jnp.bfloat16)
    grad_k = rotate(grads[1], cosine, sine, -1.0).astype(jnp.bfloat16)
    return (attended, grad_q, grad_k, grads[2].astype(jnp.bfloat16))


def solution(mesh):
    rows = P(("seq", "head"), None)
    in_specs = (rows, rows, rows, rows, P(None, "seq"), P(), P())
    out = P("seq", "head")
    return jax.shard_map(
        functools.partial(on_device, mesh.shape["seq"]),
        mesh=mesh, in_specs=in_specs, out_specs=(out,) * 4, check_vma=False,
    )
```

time: 1200 us -> 134 us (0.11)
  waiting for transfers between devices: 691 us -> 0 us
  blocking collectives: 294 us -> 0 us
  Pallas kernels: 0 us -> 120 us
  matrix products: 80.4 us -> 0 us
  loops' own time: 46.4 us -> 0 us
  local copies, waits for them, and re-layouts: 37.8 us -> 7.36 us
  starting transfers between devices: 27.6 us -> 0 us
  between operations: 13.9 us -> 0.77 us
    all_gather x4 -> x0, waiting for transfers between devices: 683 us -> none  [the longest x1 271 us: on_device(): lax.all_gather(value_split, 'seq', axis=0, tiled=True)]
    all_gather x2 -> x0, blocking collectives: 284 us -> none  [the longest x1 142 us: on_device(): lax.all_gather(level.T, 'seq', axis=0, tiled=True)]
    pallas_call x0 -> x1, Pallas kernels: none -> 120 us  [exchange_and_attend(): pl.pallas_call(functools.partial(kernel, seq_count, toks), out_shape=(jax...]
    dot_general x56 -> x0, matrix products: 80.4 us -> none  [the longest x8 14.2 us: step(): jnp.einsum('khd,qhd->hkq', key_rot, query_block, preferred_element_type=j...]
    another operation x3 -> x0, loops' own time: 46.4 us -> none  [in_blocks(): final, _ = lax.scan(advance, carry, (shaped, firsts))]
    dynamic_slice x73 -> x1, local copies, waits for them, and re-layouts: 36.4 us -> 0.07 us  [on_device(): own_pos = lax.dynamic_slice_in_dim(positions, hd * sub, sub, axis=1)]
    all_to_all x3 -> x0, starting transfers between devices: 27.4 us -> none  [the longest x1 16.5 us: on_device(): lax.all_to_all(q_in, 'head', split_axis=1, concat_axis=0, tiled=True)]
  transfers between devices with their start and end apart: 7 -> 0, of which waited for: 6 -> 0; matrix products, arithmetic and copies ran while one was open for 6% -> 0% of each run, Pallas kernels for 0% -> 0%
where the time goes in v1:
time: 134 us; the launch traced here: 132 us
  Pallas kernels  120 us (90%)
  local copies, waits for them, and re-layouts  7.36 us (5%)
  other arithmetic  3.78 us (3%)
    pallas_call x1, Pallas kernels, exchange_and_attend(): pl.pallas_call(functools.partial(kernel, seq_count, toks), out_shape=(jax...  120 us
    unnamed x13, local copies, waits for them, and re-layouts  4.13 us

profile of v1, /device:TPU:6, one launch (start us, length us, event | category | flops | bytes accessed | tf_op | source)
XLA Modules:
  0.0 131.9 jit_solution(6926826395990653892)
XLA Ops:
  0.6 0.0 copy-start.2
  0.7 0.7 copy-done.2
  1.4 0.1 slice_reduce_fusion
  1.5 0.2 select_reduce_fusion.3
  1.7 0.2 select_reduce_fusion
  1.9 0.0 copy-start.5
  1.9 0.7 copy-done.5
  2.6 0.2 select_reduce_fusion.2
  2.8 0.0 copy-start.4
  2.8 0.7 copy-done.4
  3.5 0.1 constant_dynamic-slice_fusion
  3.5 0.1 broadcast_multiply_fusion.5
  3.6 0.1 or_select_fusion
  3.7 0.1 broadcast_multiply_fusion.4
  3.8 0.1 fusion.8
  3.9 0.7 broadcast_in_dim.102
  4.6 0.0 copy-start
  4.6 0.1 broadcast_multiply_fusion.2
  4.7 0.7 copy-done
  5.3 0.7 copy-done.1
  6.1 0.1 subtract_convert_fusion.2
  6.2 0.7 maximum_bitcast_fusion
  6.9 0.1 broadcast_multiply_fusion.1
  7.0 120.0 %shard_map.102 = (bf16[128,128]{1,0:T(8,128)(2,1)}, f32[3,128,128]{2,1,0:T(8,128)}) custom-call(bf16[8,2048]{1,0:T(8,128)(2,1)} %get-tuple-element.38.k_ref, bf16[8,2048]{1,0:T(8,128)(2,1)} %v_ref.1, bf16[8,2048]{1,0:T(8,128)(2,1)} %get-tuple-element.39.q_ref, bf16[8,2048]{1,0:T(8,128)(2,1)} %d_ref.1, f32[16,1,512]{2,1,0:T(1,128)} %bitcast.34), custom_call_target="tpu_custom_call" | custom-call | tf_op jit(solution)/shard_map/pallas_call | solution.py:503
  127.0 1.5 %fusion = bf16[128,128]{1,0:T(8,128)(2,1)} fusion(f32[3,128,128]{2,1,0:T(8,128)} %get-tuple-element.7), kind=kLoop, calls=%fused_computation.12 | loop fusion | bytes 65536 | tf_op jit(solution)/shard_map/convert_element_type | solution.py:582
  128.5 0.9 slice_bitcast_fusion.1
  129.3 0.3 subtract_convert_fusion
  129.7 0.1 subtract_convert_fusion.1
  129.8 0.7 pad_maximum_fusion.2
  130.5 0.7 pad_maximum_fusion.1
  131.2 0.1 copy-done.3
  131.3 0.6 copy.12
  (11 shorter events, 0.1 us)
Async XLA Ops:
  0.6 0.8 copy-start.2
  1.9 0.7 copy-start.5
  2.8 0.7 copy-start.4
  4.6 0.8 copy-start
  5.3 0.8 copy-start.1
  130.5 0.8 copy-start.3

commit v2 on v1

--- a/solution.py
+++ b/solution.py
@@ -2,6 +2,7 @@
 
 import jax
 import jax.numpy as jnp
+import numpy as np
 from jax import lax
 from jax.experimental import pallas as pl
 from jax.experimental.pallas import tpu as pltpu
@@ -12,27 +13,7 @@
 THETA = 10000.0
 MESH = pl.DeviceIdType.MESH
 SKEW = 1
-
-
-def rope_tables(positions, width):
-    side = width // 6 * 2
-    first = width - 2 * side
-    parts = []
-    for row, group in ((0, first), (1, side), (2, side)):
-        steps = jnp.arange(group // 2, dtype=jnp.float32)
-        inverse = THETA ** (-2.0 * steps / group)
-        parts.append(positions[row].astype(jnp.float32)[:, None] * inverse[None, :])
-    angles = jnp.concatenate(parts, axis=1)
-    return (jnp.cos(angles), jnp.sin(angles))
-
-
-def rotate(values, cosine, sine, sign):
-    half = values.shape[-1] // 2
-    first = values[..., :half]
-    second = values[..., half:]
-    return jnp.concatenate(
-        [first * cosine - sign * second * sine, sign * first * sine + second * cosine], axis=-1
-    )
+PIECES = 4
 
 
 def dot_nt(a, b):
@@ -49,9 +30,10 @@
 
 def kernel(
     seq_count, toks,
-    k_ref, v_ref, q_ref, d_ref, bias_ref,
-    att_ref, grad_ref,
-    ring, gbuf, acc, stat, racc, rstat, lring, glse, dqt, dkv, attbuf, hsend, hrecv,
+    k_hbm, v_ref, q_hbm, d_ref, pos_hbm, views_hbm, adj_ref, freq_ref,
+    out_ref,
+    k_raw, q_raw, k_ref, q_ref, pos_ref, views_ref, bias_ref, ctab, stab, in_sem,
+    ring, gbuf, acc, pbuf, stat, racc, rstat, lring, glse, dqt, dkv, attbuf, hsend, hrecv,
     a2a_send, a2a_recv, g_send, g_recv, g_own, r_send, r_recv, l_send, l_recv,
     p_send, p_recv, gl_send, gl_recv, gl_own, at_send, at_recv, h_send, h_recv,
 ):
@@ -92,6 +74,15 @@
     def is_me(dev):
         return jnp.logical_and(dev[0] == s, dev[1] == hd)
 
+    loads = [
+        pltpu.make_async_copy(src, dst, in_sem.at[n])
+        for n, (src, dst) in enumerate(
+            ((pos_hbm, pos_ref), (views_hbm, views_ref), (k_hbm, k_raw), (q_hbm, q_raw))
+        )
+    ]
+    for load in loads:
+        load.start()
+
     barrier = pltpu.get_barrier_semaphore()
 
     @pl.loop(0, 16)
@@ -109,14 +100,56 @@
         def _():
             pl.semaphore_signal(barrier, inc=1, device_id=src, device_id_type=MESH)
 
-    for dev in (right, left):
+    far_right = ((s + 8) % seq_count, hd)
+    far_left = ((s + seq_count - 8) % seq_count, hd)
+    for dev in (right, left, far_right, far_left):
         pl.semaphore_signal(barrier, inc=1, device_id=dev, device_id_type=MESH)
     peers = []
     for delta in (1, 2, 3):
         i = (j + delta) % 4
         peers.append(i)
         pl.semaphore_signal(barrier, inc=1, device_id=member((j - delta + 4) % 4), device_id_type=MESH)
-    pl.semaphore_wait(barrier, 25 - 2 * diag.astype(jnp.int32))
+
+    loads[0].wait()
+    spots = pos_ref[...].astype(jnp.float32)
+    spots = jnp.transpose(jnp.concatenate([spots, jnp.zeros((5, T), jnp.float32)], axis=0))
+    lane = lax.broadcasted_iota(jnp.int32, (T, HD), 1)
+    within = lane % (HD // 2)
+    side = HD // 6 * 2 // 2
+    first = HD // 2 - 2 * side
+    spot = jnp.where(
+        within < first, spots[:, 0:1], jnp.where(within < first + side, spots[:, 1:2], spots[:, 2:3])
+    )
+    angle = spot * freq_ref[...]
+    ctab[...] = jnp.cos(angle)
+    sine = jnp.sin(angle)
+    stab[...] = jnp.where(lane < HD // 2, -sine, sine)
+    own_rows = pl.ds(pl.multiple_of(hd * SUB, SUB), SUB)
+    c_own = ctab[own_rows, :]
+    s_own = stab[own_rows, :]
+    for n, src, dst in ((2, k_raw, k_ref), (3, q_raw, q_ref)):
+        loads[n].wait()
+        for h in range(16):
+            x = src[:, h * HD:(h + 1) * HD].astype(jnp.float32)
+            y = x * c_own + pltpu.roll(x, HD // 2, 1) * s_own
+            dst[:, h * HD:(h + 1) * HD] = y.astype(jnp.bfloat16)
+    loads[1].wait()
+    views_q = [views_ref[base + i] for i in range(4)]
+    nears = []
+    for vq in views_q:
+        one = jnp.zeros_like(vq)
+        two = jnp.zeros_like(vq)
+        for v in range(6):
+            one = jnp.where(vq == v, adj_ref[0, v], one)
+            two = jnp.where(vq == v, adj_ref[1, v], two)
+        nears.append((one, two))
+    for slot in range(NP):
+        offset = -((slot + 1) // 2) if slot % 2 else slot // 2
+        vk = views_ref[(pair + offset + NP) % NP * 4 + j]
+        for i in range(4):
+            allow = (vk == views_q[i]) | (vk == nears[i][0]) | (vk == nears[i][1])
+            bias_ref[slot, :, i * T:(i + 1) * T] = jnp.where(allow, 0.0, NEG)
+    pl.semaphore_wait(barrier, 27 - 2 * diag.astype(jnp.int32))
 
     inputs = (k_ref, v_ref, q_ref, d_ref)
 
@@ -157,7 +190,9 @@
     def wait_bytes(ref, sem):
         pltpu.make_async_copy(ref, ref, sem).wait()
 
-    def ring_copy(t, way, step):
+    PT = T // PIECES
+
+    def ring_copy(t, way, step, piece):
         if way == 0:
             src = jnp.maximum(2 * step - 3, 0)
             dst = 2 * step - 1
@@ -165,23 +200,32 @@
             src = 2 * step - 2
             dst = jnp.minimum(2 * step, 2 * HALF - 1)
         return pltpu.make_async_remote_copy(
-            src_ref=ring.at[t, pl.ds(pl.multiple_of(src * T, T), T), :],
-            dst_ref=ring.at[t, pl.ds(pl.multiple_of(dst * T, T), T), :],
-            send_sem=r_send.at[t, way, step - 1], recv_sem=r_recv.at[t, way, step - 1],
+            src_ref=ring.at[t, pl.ds(pl.multiple_of(src * T + piece * PT, PT), PT), :],
+            dst_ref=ring.at[t, pl.ds(pl.multiple_of(dst * T + piece * PT, PT), PT), :],
+            send_sem=r_send.at[t, way], recv_sem=r_recv.at[t, way, (step - 1) * PIECES + piece],
             device_id=right if way == 0 else left, device_id_type=MESH,
         )
 
+    def ring_start(tensors):
+        for piece in range(PIECES):
+            for t in tensors:
+                for way in (0, 1):
+                    ring_copy(t, way, jnp.int32(1), piece).start()
+
+    def ring_last(t):
+        for piece in range(PIECES):
+            ring_copy(t, t % 2, jnp.int32(HALF), piece).wait_recv()
+
     def lse_copy(way, step):
-        if way == 0:
-            src = jnp.maximum(2 * step - 3, 0)
-            dst = 2 * step - 1
-        else:
-            src = 2 * step - 2
-            dst = jnp.minimum(2 * step, 2 * HALF - 1)
-        return pltpu.make_async_remote_copy(
-            src_ref=lring.at[src], dst_ref=lring.at[dst],
+        slot = 2 * step - 1 if way == 0 else jnp.minimum(2 * step, 2 * HALF - 1)
+        back = jnp.maximum(step - 2, 0)
+        src = jnp.maximum(2 * back - 1, 0) if way == 0 else 2 * back
+        stride = 4 * jnp.minimum(step, 2)
+        seq = (s + stride) % seq_count if way == 0 else (s + seq_count - stride) % seq_count
+        return pltpu.make_async_remote_copy(
+            src_ref=lring.at[src], dst_ref=lring.at[slot],
             send_sem=l_send.at[way, step - 1], recv_sem=l_recv.at[way, step - 1],
-            device_id=right if way == 0 else left, device_id_type=MESH,
+            device_id=(seq, hd), device_id_type=MESH,
         )
 
     def group_copy(t, n):
@@ -198,8 +242,7 @@
 
     for t in (0, 1):
         wait_bytes(own(t), a2a_recv.at[t])
-        for way in (0, 1):
-            ring_copy(t, way, jnp.int32(1)).start()
+    ring_start((0, 1))
     for t in (2, 3):
         wait_bytes(own(t), a2a_recv.at[t])
     for t in (2, 3, 0, 1):
@@ -246,41 +289,46 @@
     fwd(0, T, bias_ref[0], True)
 
     def forward_ring(pairs, step):
-        for t, way in pairs:
-            ring_copy(t, way, step).wait_recv()
-
-            @pl.when(step + 1 < HALF)
-            def _():
-                ring_copy(t, way, step + 1).start()
-
-            if (t % 2) == way:
-                @pl.when(step + 1 == HALF)
+        for piece in range(PIECES):
+            for t, way in pairs:
+                ring_copy(t, way, step, piece).wait_recv()
+
+                @pl.when(step + 1 < HALF)
                 def _():
-                    ring_copy(t, way, step + 1).start()
+                    ring_copy(t, way, step + 1, piece).start()
+
+                if (t % 2) == way:
+                    @pl.when(step + 1 == HALF)
+                    def _():
+                        ring_copy(t, way, step + 1, piece).start()
 
     @pl.loop(1, HALF)
     def _(step):
         forward_ring(((0, 0), (0, 1), (1, 0), (1, 1)), step)
+
+        @pl.when(step + 1 == HALF)
+        def _():
+            ring_start((2, 3))
+
         fwd(pl.multiple_of((2 * step - 1) * T, T), 2 * T, bias_of(step), False)
 
-    for t in (2, 3):
-        for way in (0, 1):
-            ring_copy(t, way, jnp.int32(1)).start()
-    ring_copy(0, 0, jnp.int32(HALF)).wait_recv()
-    ring_copy(1, 1, jnp.int32(HALF)).wait_recv()
+    ring_last(0)
+    ring_last(1)
     fwd(LAST * T, T, bias_ref[LAST], False)
 
     def part_copy(which, n):
         lanes = pl.ds(pl.multiple_of(peers[n] * T, T), T)
-        src, dst = ((acc, racc), (stat, rstat))[which]
+        src, dst = ((pbuf, racc), (stat, rstat))[which]
         return pltpu.make_async_remote_copy(
             src_ref=src.at[:, lanes], dst_ref=dst.at[n],
             send_sem=p_send.at[which, n], recv_sem=p_recv.at[which, n],
             device_id=member(peers[n]), device_id_type=MESH,
         )
 
+    pbuf[...] = acc[...].astype(jnp.bfloat16)
     for n in range(3):
         part_copy(1, n).start()
+    for n in range(3):
         part_copy(0, n).start()
     for t in (3, 0, 1):
         group_wait(t)
@@ -299,7 +347,7 @@
     for n, item in enumerate(stats):
         weight = jnp.exp(item[0:1] - top)
         total = total + item[1:2] * weight
-        out = out + (own_acc if n == 0 else racc[n - 1]) * weight
+        out = out + (own_acc if n == 0 else racc[n - 1].astype(jnp.float32)) * weight
     out = out / total
     lse = top + jnp.log(total)
     dt = jnp.transpose(ring[3, 0:T, :].astype(jnp.float32))
@@ -308,8 +356,9 @@
     lring[0, 1:2, :] = delta
     lring[0, 2:8, :] = jnp.zeros((6, T), jnp.float32)
     attbuf[...] = jnp.transpose(out).astype(jnp.bfloat16)
-    for way in (0, 1):
-        lse_copy(way, jnp.int32(1)).start()
+    for step in (1, 2):
+        for way in (0, 1):
+            lse_copy(way, jnp.int32(step)).start()
 
     def glse_copy(n):
         return pltpu.make_async_remote_copy(
@@ -325,11 +374,11 @@
 
     def att_remote():
         return pltpu.make_async_remote_copy(
-            src_ref=attbuf, dst_ref=att_ref, send_sem=at_send, recv_sem=at_recv,
+            src_ref=attbuf, dst_ref=out_ref.at[0], send_sem=at_send, recv_sem=at_recv,
             device_id=home(j), device_id_type=MESH,
         )
 
-    att_local = pltpu.make_async_copy(attbuf, att_ref, at_recv)
+    att_local = pltpu.make_async_copy(attbuf, out_ref.at[0], at_recv)
     att_mine = is_me(home(j))
 
     @pl.when(att_mine)
@@ -397,13 +446,13 @@
             for way in (0, 1):
                 lse_copy(way, at).wait_recv()
 
-                @pl.when(at + 1 < HALF)
+                @pl.when(at + 2 < HALF)
                 def _():
-                    lse_copy(way, at + 1).start()
-
-            @pl.when(at + 1 == HALF)
+                    lse_copy(way, at + 2).start()
+
+            @pl.when(at + 2 == HALF)
             def _():
-                lse_copy(0, at + 1).start()
+                lse_copy(0, at + 2).start()
 
             grad_q(pl.multiple_of((2 * at - 1) * T, T), 2 * T, bias_of(at), False)
             grad_kv(2 * at - 1, False)
@@ -437,8 +486,8 @@
                 home_remote(t, i).start()
 
     send_home(0)
-    ring_copy(2, 0, jnp.int32(HALF)).wait_recv()
-    ring_copy(3, 1, jnp.int32(HALF)).wait_recv()
+    ring_last(2)
+    ring_last(3)
     lse_copy(0, jnp.int32(HALF)).wait_recv()
     grad_kv(LAST, False)
     hsend[1] = (dkv[0] * scale).astype(jnp.bfloat16)
@@ -459,9 +508,11 @@
         @pl.loop(1, HALF)
         def _(step):
             for way in (0, 1):
-                ring_copy(t, way, step).wait_send()
-
-        ring_copy(t, t % 2, jnp.int32(HALF)).wait_send()
+                for piece in range(PIECES):
+                    ring_copy(t, way, step, piece).wait_send()
+
+        for piece in range(PIECES):
+            ring_copy(t, t % 2, jnp.int32(HALF), piece).wait_send()
 
     @pl.loop(1, HALF)
     def _(step):
@@ -478,14 +529,16 @@
     def _():
         att_remote().wait_send()
 
-    wait_bytes(att_ref, at_recv)
+    wait_bytes(out_ref.at[0], at_recv)
     for t in range(3):
         for i in range(4):
             wait_bytes(hrecv.at[t, i], h_recv.at[t, i])
         whole = hrecv[t, 0].astype(jnp.float32)
         for i in range(1, 4):
             whole = whole + hrecv[t, i].astype(jnp.float32)
-        grad_ref[t] = whole
+        if t < 2:
+            whole = whole * ctab[...] - pltpu.roll(whole, HD // 2, 1) * stab[...]
+        out_ref[t + 1] = whole.astype(jnp.bfloat16)
     for t in range(3):
         for i in range(4):
             @pl.when(jnp.logical_not(is_me(home(i))))
@@ -493,27 +546,41 @@
                 home_remote(t, i).wait_send()
 
 
-def exchange_and_attend(seq_count, toks, keys, values, query, grads, bias):
+def exchange_and_attend(seq_count, toks, keys, values, query, grads, positions, views, adjacency):
     NP = seq_count // 4
     HALF = NP // 2
     T = toks
-    bf, f32 = jnp.bfloat16, jnp.float32
+    bf, f32, i32 = jnp.bfloat16, jnp.float32, jnp.int32
+    sub = keys.shape[0]
     dma = pltpu.SemaphoreType.DMA
     vmem = pl.BlockSpec(memory_space=pltpu.VMEM)
+    smem = pl.BlockSpec(memory_space=pltpu.SMEM)
+    anywhere = pl.BlockSpec(memory_space=pl.ANY)
+    side = HD // 6 * 2
+    parts = []
+    for group in (HD - 2 * side, side, side):
+        steps = np.arange(group // 2, dtype=np.float32)
+        parts.append(np.float32(THETA) ** (np.float32(-2.0) * steps / np.float32(group)))
+    freq = jnp.asarray(np.concatenate(parts * 2).astype(np.float32)[None])
     return pl.pallas_call(
         functools.partial(kernel, seq_count, toks),
-        out_shape=(
-            jax.ShapeDtypeStruct((T, HD), bf),
-            jax.ShapeDtypeStruct((3, T, HD), f32),
-        ),
-        in_specs=[vmem] * 5,
-        out_specs=(vmem, vmem),
+        out_shape=jax.ShapeDtypeStruct((4, T, HD), bf),
+        in_specs=[anywhere] * 6 + [smem, vmem],
+        out_specs=vmem,
         scratch_shapes=[
+            pltpu.VMEM(keys.shape, bf), pltpu.VMEM(keys.shape, bf),
+            pltpu.VMEM(keys.shape, bf), pltpu.VMEM(keys.shape, bf),
+            pltpu.VMEM(positions.shape, i32),
+            pltpu.VMEM((seq_count, 1, T), i32),
+            pltpu.VMEM((NP, 1, 4 * T), f32),
+            pltpu.VMEM((T, HD), f32), pltpu.VMEM((T, HD), f32),
+            dma((4,)),
             pltpu.VMEM((4, NP * T, HD), bf),
             pltpu.VMEM((4, 4 * T, HD), bf),
             pltpu.VMEM((HD, 4 * T), f32),
+            pltpu.VMEM((HD, 4 * T), bf),
             pltpu.VMEM((8, 4 * T), f32),
-            pltpu.VMEM((3, HD, T), f32),
+            pltpu.VMEM((3, HD, T), bf),
             pltpu.VMEM((3, 8, T), f32),
             pltpu.VMEM((NP, 8, T), f32),
             pltpu.VMEM((8, 4 * T), f32),
@@ -524,7 +591,7 @@
             pltpu.VMEM((3, 4, T, HD), bf),
             dma((4,)), dma((4,)),
             dma((4, 3)), dma((4, 3)), dma((4,)),
-            dma((4, 2, HALF)), dma((4, 2, HALF)),
+            dma((4, 2)), dma((4, 2, HALF * PIECES)),
             dma((2, HALF)), dma((2, HALF)),
             dma((2, 3)), dma((2, 3)),
             dma((3,)), dma((3,)), dma,
@@ -532,54 +599,16 @@
             dma((3, 4)), dma((3, 4)),
         ],
         compiler_params=pltpu.CompilerParams(collective_id=0, has_side_effects=True),
-    )(keys, values, query, grads, bias)
+    )(keys, values, query, grads, positions, views, adjacency, freq)
 
 
 def on_device(seq_count, q_in, k_in, v_in, grad_out, positions, views, adjacency):
-    NP = seq_count // 4
-    HALF = NP // 2
     T = positions.shape[1]
-    sub = q_in.shape[0]
-    s = lax.axis_index("seq")
-    hd = lax.axis_index("head")
-    cosine, sine = rope_tables(positions, HD)
-    own_pos = lax.dynamic_slice_in_dim(positions, hd * sub, sub, axis=1)
-    c8, s8 = rope_tables(own_pos, HD)
-
-    def turn(x):
-        y = rotate(x.reshape(sub, -1, HD).astype(jnp.float32), c8[:, None], s8[:, None], 1.0)
-        return y.astype(jnp.bfloat16).reshape(x.shape)
-
-    pair = s // 4
-    j = 2 * (hd // 8) + s % 2
-    step = jnp.arange(NP, dtype=jnp.int32)
-    offset = jnp.where(step % 2 == 1, -(step + 1) // 2, step // 2)
-    other = (pair + offset + NP) % NP * 4 + j
-    mine = 4 * pair + jnp.arange(4, dtype=jnp.int32)
-    block_views = views.reshape(seq_count, T)[:, 0]
-    every = jnp.arange(seq_count, dtype=jnp.int32)
-
-    def view_of(index):
-        return jnp.sum(jnp.where(index[:, None] == every[None, :], block_views[None, :], 0), axis=1)
-
-    key_view = view_of(other)
-    own_view = view_of(mine)
-    match = own_view[:, None] == jnp.arange(adjacency.shape[0], dtype=jnp.int32)[None, :]
-    near_one = jnp.sum(jnp.where(match, adjacency[None, :, 0], 0), axis=1)
-    near_two = jnp.sum(jnp.where(match, adjacency[None, :, 1], 0), axis=1)
-    allow = (
-        (key_view[:, None] == own_view[None, :])
-        | (key_view[:, None] == near_one[None, :])
-        | (key_view[:, None] == near_two[None, :])
+    out = exchange_and_attend(
+        seq_count, T, k_in, v_in, q_in, grad_out,
+        positions, views.reshape(seq_count, 1, T), adjacency.T,
     )
-    bias = jnp.broadcast_to(jnp.where(allow, 0.0, NEG)[:, :, None], (NP, 4, T)).reshape(NP, 1, 4 * T)
-
-    attended, grads = exchange_and_attend(
-        seq_count, T, turn(k_in), v_in, turn(q_in), grad_out, bias
-    )
-    grad_q = rotate(grads[0], cosine, sine, -1.0).astype(jnp.bfloat16)
-    grad_k = rotate(grads[1], cosine, sine, -1.0).astype(jnp.bfloat16)
-    return (attended, grad_q, grad_k, grads[2].astype(jnp.bfloat16))
+    return (out[0], out[1], out[2], out[3])
 
 
 def solution(mesh):

time: 134 us -> 114 us (0.85); the launches traced: 132 us -> 113 us
  Pallas kernels: 120 us -> 111 us
  local copies, waits for them, and re-layouts: 7.36 us -> 1.46 us
  other arithmetic: 3.78 us -> 0 us
    pallas_call x1, Pallas kernels: 120 us -> 111 us  [exchange_and_attend(): pl.pallas_call(functools.partial(kernel, seq_count, toks), out_shape=jax....]
    unnamed x13 -> x0, local copies, waits for them, and re-layouts: 4.13 us -> none
    convert_element_type x1 -> x0, local copies, waits for them, and re-layouts: 1.46 us -> none  [on_device(): return (attended, grad_q, grad_k, grads[2].astype(jnp.bfloat16))]
    concatenate x2 -> x0, other arithmetic: 1.4 us -> none  [rotate(): jnp.concatenate([first * cosine - sign * second * sine, sign * first * si...]
where the time goes in v2:
time: 114 us; the launch traced here: 113 us
  Pallas kernels  111 us (97%)
  local copies, waits for them, and re-layouts  1.46 us (1%)
    pallas_call x1, Pallas kernels, exchange_and_attend(): pl.pallas_call(functools.partial(kernel, seq_count, toks), out_shape=jax....  111 us

profile of v2, /device:TPU:6, one launch (start us, length us, event | category | flops | bytes accessed | tf_op | source)
XLA Modules:
  0.0 113.3 jit_solution(9163772445552089971)
XLA Ops:
  0.6 111.2 %shard_map.111 = bf16[4,128,128]{2,1,0:T(8,128)(2,1)} custom-call(bf16[8,2048]{1,0:T(8,128)(2,1)} %k_hbm.1, bf16[8,2048]{1,0:T(8,128)(2,1)} %v_ref.1, bf16[8,2048]{1,0:T(8,128)(2,1)} %q_hbm.1, bf16[8,2048]{1,0:T(8,128)(2,1)} %d_ref.1, s32[3,128]{1,0:T(4,128)} %pos_hbm.1, s32[64,1,128]{2,1,0:T(1,128)} %bitcast.10, s32[2,6]{1,0:T(2,128)} %bitcast.11, ...), custom_call_target="tpu_custom_call" | custom-call | tf_op jit(solution)/shard_map/pallas_call | solution.py:565
  111.8 1.5 %slice_bitcast_fusion = (bf16[128,128]{1,0:T(8,128)(2,1)}, bf16[128,128]{1,0:T(8,128)(2,1)}, bf16[128,128]{1,0:T(8,128)(2,1)}, bf16[128,128]{1,0:T(8,128)(2,1)}) fusion(bf16[4,128,128]{2,1,0:T(8,128)(2,1)} %shard_map.111), kind=kLoop, calls=%fused_computation | loop fusion | bytes 262144 | tf_op jit(solution)/shard_map/squeeze | solution.py:611
